TPU v7x, 512 devices: a whole 4x8x8 slice. The times are simulated.
512 devices in a mesh: seq: 16 (over z, core), dp: 8 (over y), mp: 4 (over x).
Axes of the slice: x: 4, y: 8, z: 8, core: 2. Of those that a mesh axis runs over, the one named last changes fastest.
Arguments:
- features: bfloat16 [8, 4096, 8, 512], P('dp', 'seq', None, 'mp'), may hold values from -6 to 6
- key_projection: bfloat16 [8, 4096, 8, 128], P('dp', 'seq'), may hold values from -2 to 2
- query_proj: bfloat16 [8, 4096, 8, 128], P('dp', 'seq'), may hold values from -2 to 2
- step_raw: float32 [8, 4096, 8, 8], P('dp', 'seq', None, 'mp'), may hold values from -3 to 6
- doc_starts: int32 [8, 4096], P('dp', 'seq'), may hold values 0 or 1
- log_rate: float32 [8, 8], P(None, 'mp'), may hold values from -5 to 1
- step_bias: float32 [8, 8], P(None, 'mp'), may hold values from -5 to -2.5
- skip_gain: float32 [8, 8], P(None, 'mp'), may hold values from 0.5 to 1.5
- out_grad: bfloat16 [8, 4096, 8, 512], P('dp', 'seq', None, 'mp'), may hold values from -6 to 6
Outputs:
- mixed_out: bfloat16 [8, 4096, 8, 512], P('dp', 'seq', None, 'mp')
- features_grad: bfloat16 [8, 4096, 8, 512], P('dp', 'seq', None, 'mp')
- key_grad: bfloat16 [8, 4096, 8, 128], P('dp', 'seq', 'mp')
- query_grad: bfloat16 [8, 4096, 8, 128], P('dp', 'seq', 'mp')
- step_grad: float32 [8, 4096, 8, 8], P('dp', 'seq', None, 'mp')
- log_rate_grad: float32 [8, 8], P(None, 'mp')
- step_bias_grad: float32 [8, 8], P(None, 'mp')
- skip_grad: float32 [8, 8], P(None, 'mp')
All inputs are finite; a program needn't handle non-finite values. No bound on the sum of `doc_starts` on one device may be relied on, other than what follows from the above.
Results may differ from a plain program's by a relative error of at most 0.0015.
Values sent between devices are 32-bit elements; how exact they have to be, the bound alone decides.
No kernel may reach another device: no remote copies, remote signals or barrier semaphores. Data moves between devices by JAX's collectives and lax.ppermute only.
A program may use at most 128 MiB of HBM per device.

v0:
```python
import functools

import jax
import jax.numpy as jnp
from jax import lax
from jax.experimental import pallas as pl
from jax.experimental.pallas import tpu as pltpu
from jax.sharding import PartitionSpec as P


P_SIZE = 64
N = 128
F32 = jnp.float32
BF16 = jnp.bfloat16
NN = (((1,), (0,)), ((), ()))
NT = (((1,), (1,)), ((), ()))
TN = (((0,), (0,)), ((), ()))


def dot(a, b, dims=NN):
    return lax.dot_general(a, b, dims, preferred_element_type=F32)


def split(a):
    high = a.astype(BF16)
    return high, (a - high.astype(F32)).astype(BF16)


def exact_dot(a, b):
    return lax.dot_general(
        a, b, NN, precision=lax.Precision.HIGHEST, preferred_element_type=F32
    )


def softplus(v):
    u = jnp.exp(-jnp.abs(v))
    series = u * (1.0 + u * (-1.0 / 2 + u * (1.0 / 3 + u * (-1.0 / 4 + u * (1.0 / 5)))))
    return jnp.maximum(v, 0.0) + jnp.where(u < 0.03, series, jnp.log(1.0 + u))


def pair_rows(ref, pairs, length):
    half = pairs // 2
    rows = [jnp.full((1, length), ref[j // half, j % half], F32) for j in range(pairs)]
    return jnp.concatenate(rows, axis=0)


def row_of(base, g, h):
    return pl.ds(base + 8 * h + g, 1)


def two_heads(rows_ref, base, g, length):
    top, low = rows_ref[row_of(base, g, 0), :], rows_ref[row_of(base, g, 1), :]
    return jnp.concatenate(
        [jnp.broadcast_to(top, (P_SIZE, length)), jnp.broadcast_to(low, (P_SIZE, length))], axis=0
    )


CUM, DT, ENTRY, TAIL, SIG, LOGD, DOC = 0, 16, 32, 48, 64, 80, 96
ROWS = 104


def summary_kernel(
    x_hbm, dy_hbm, b_hbm, c_hbm, raw_hbm, doc_hbm, rate_hbm, bias_hbm,
    keep_ref, give_ref, rows_ref,
    xs, ys, bs, cs, x_in, dy_in, b_in, c_in, raw_ref, doc_ref, rate_ref, bias_ref, sems,
):
    length, groups, _ = x_hbm.shape
    loads = [
        pltpu.make_async_copy(src, dst, sems.at[k])
        for k, (src, dst) in enumerate((
            (raw_hbm, raw_ref), (doc_hbm, doc_ref), (rate_hbm, rate_ref), (bias_hbm, bias_ref),
            (x_hbm, x_in), (dy_hbm, dy_in), (b_hbm, b_in), (c_hbm, c_in),
        ))
    ]
    for load in loads:
        load.start()
    for load in loads[:4]:
        load.wait()
    pairs = 2 * groups
    core = core_of_chip()
    raw = jnp.concatenate(
        [raw_ref[g, h : h + 1, :] for h in range(2) for g in range(groups)], axis=0
    )
    shifted = raw + pair_rows(bias_ref, pairs, length)
    dt = softplus(shifted)
    log_decay = -dt * jnp.exp(pair_rows(rate_ref, pairs, length))
    docs = jnp.broadcast_to(doc_ref[...].astype(F32), (8, length))
    before = lax.broadcasted_iota(jnp.int32, (length, length), 0)
    after = lax.broadcasted_iota(jnp.int32, (length, length), 1)
    upto = jnp.where(before <= after, 1.0, 0.0).astype(F32)
    sums = exact_dot(jnp.concatenate([log_decay, docs], axis=0), upto)
    cum = sums[:pairs]
    count = sums[pairs : pairs + 1]
    last = cum[:, length - 1 :]
    last_count = count[:, length - 1 :]
    entry = jnp.where(count == 0.0, jnp.exp(cum), 0.0)
    tail = jnp.where(count == last_count, jnp.exp(last - cum), 0.0) * dt
    rows_ref[CUM : CUM + 16] = cum
    rows_ref[DT : DT + 16] = dt
    rows_ref[ENTRY : ENTRY + 16] = entry
    rows_ref[TAIL : TAIL + 16] = tail
    rows_ref[SIG : SIG + 16] = 1.0 / (1.0 + jnp.exp(-shifted))
    rows_ref[LOGD : LOGD + 16] = log_decay
    rows_ref[DOC : DOC + 8] = jnp.broadcast_to(count, (8, length))
    for load, src, dst in zip(loads[4:], (x_in, dy_in, b_in, c_in), (xs, ys, bs, cs)):
        load.wait()
        dst[...] = src[...].astype(F32).reshape(length * groups, 128)

    def totals_of(g):
        x_t = xs[pl.ds(g, length, stride=groups), :].T
        dy_t = ys[pl.ds(g, length, stride=groups), :].T
        b_n = bs[pl.ds(g, length, stride=groups), :].astype(BF16)
        c_n = cs[pl.ds(g, length, stride=groups), :].astype(BF16)
        totals = []
        for vals, weights, other in ((x_t, TAIL, b_n), (dy_t, ENTRY, c_n)):
            high, low = split(vals * two_heads(rows_ref, weights, g, length))
            both = dot(jnp.concatenate([high, low], axis=0), other)
            totals.append(both[:128] + both[128:])
        return totals

    half = groups // 2
    passed = entry[:, length - 1 :]
    for i in range(half):
        low, high = totals_of(i), totals_of(half + i)
        for h in range(2):
            part = slice(h * P_SIZE, (h + 1) * P_SIZE)
            for at, a, b in zip((0, P_SIZE), low, high):
                keep_ref[2 * i + h, at : at + P_SIZE] = jnp.where(core == 0, a[part], b[part])
                give_ref[2 * i + h, at : at + P_SIZE] = jnp.where(core == 0, b[part], a[part])
            a = jnp.broadcast_to(passed[groups * h + i : groups * h + i + 1], (8, N))
            b = jnp.broadcast_to(passed[groups * h + half + i : groups * h + half + i + 1], (8, N))
            keep_ref[2 * i + h, 2 * P_SIZE :] = jnp.where(core == 0, a, b)
            give_ref[2 * i + h, 2 * P_SIZE :] = jnp.where(core == 0, b, a)


def core_of_chip():
    return lax.rem(lax.axis_index("seq"), 2)


def state_of(ref, k):
    return ref[k, :P_SIZE]


def adjoint_of(ref, k):
    return ref[k, P_SIZE : 2 * P_SIZE]


def passed_of(ref, k):
    return ref[k, 2 * P_SIZE : 2 * P_SIZE + 1, :]


def chip_kernel(keep_ref, got_ref, chip_ref):
    def join(first, second):
        for k in range(chip_ref.shape[0]):
            chip_ref[k, :P_SIZE] = passed_of(second, k) * state_of(first, k) + state_of(second, k)
            chip_ref[k, P_SIZE : 2 * P_SIZE] = adjoint_of(first, k) + passed_of(
                first, k
            ) * adjoint_of(second, k)
            chip_ref[k, 2 * P_SIZE :] = first[k, 2 * P_SIZE :] * second[k, 2 * P_SIZE :]

    core = core_of_chip()
    pl.when(core == 0)(lambda: join(keep_ref, got_ref))
    pl.when(core == 1)(lambda: join(got_ref, keep_ref))


def scan_kernel(recv_ref, send_ref):
    chips = recv_ref.shape[0]
    state = jnp.zeros((P_SIZE, N), F32)
    for k in range(chips):
        send_ref[k, :P_SIZE] = state
        if k < chips - 1:
            state = passed_of(recv_ref, k) * state + state_of(recv_ref, k)
    state = jnp.zeros((P_SIZE, N), F32)
    for k in reversed(range(chips)):
        send_ref[k, P_SIZE:] = state
        if k > 0:
            state = passed_of(recv_ref, k) * state + adjoint_of(recv_ref, k)


def states_of(refs, g, groups, at):
    core = core_of_chip()
    mine = g // (groups // 2) == core
    through = core == (1 if at == 0 else 0)
    slot = 2 * lax.rem(g, groups // 2)
    ends_mine, ends_other, sums_mine, sums_other = refs
    part = slice(at, at + P_SIZE)
    states = []
    for k in (slot, slot + 1):
        end = jnp.where(mine, ends_mine[k, part], ends_other[k, part])
        summary = jnp.where(mine, sums_mine[k, part], sums_other[k, part])
        passed = jnp.where(mine, passed_of(sums_mine, k), passed_of(sums_other, k))
        states.append(jnp.where(through, passed * end + summary, end))
    return states


def within_kernel(
    start,
    x_ref, dy_ref, b_ref, c_ref, rows_ref,
    *rest,
):
    yt_ref, dxt_ref, dct_ref, dbt_ref, xt_ref, dyt_ref, bt_ref, ct_ref, xs, ys, bs, cs = rest[-12:]
    groups, _, length = yt_ref.shape
    stride = x_ref.shape[1]
    for src, dst in ((x_ref, xs), (dy_ref, ys), (b_ref, bs), (c_ref, cs)):
        dst[...] = src[...].astype(F32).reshape(length * stride, 128)
    t_at = lax.broadcasted_iota(jnp.int32, (length, length), 0)
    s_at = lax.broadcasted_iota(jnp.int32, (length, length), 1)
    count = rows_ref[DOC : DOC + 8]
    count_col = count.T[:, :1]
    far = jnp.where((t_at >= s_at) & (count_col == count[:1]), 0.0, -jnp.inf)
    lanes = lax.broadcasted_iota(jnp.int32, (length, 128), 1)

    def group(i, carry):
        g = start + i
        x_n, dy_n, b_n, c_n = (
            ref[pl.ds(g, length, stride=stride), :] for ref in (xs, ys, bs, cs)
        )
        b_t, c_t = b_n.T.astype(BF16), c_n.T.astype(BF16)
        c_n, dy_n, x_t = c_n.astype(BF16), dy_n.astype(BF16), x_n.T.astype(BF16)
        bt_ref[i] = b_t
        ct_ref[i] = c_t
        xt_ref[i] = x_t
        dyt_ref[i] = dy_n.T
        scores = dot(c_n, b_t)
        cum = jnp.concatenate(
            [rows_ref[row_of(CUM, g, 0), :], rows_ref[row_of(CUM, g, 1), :]]
            + [jnp.zeros((6, length), F32)],
            axis=0,
        )
        cum_col = cum.T
        score_grad = None
        for h in range(2):
            part = slice(h * P_SIZE, (h + 1) * P_SIZE)
            dt = rows_ref[row_of(DT, g, h), :]
            weight = jnp.exp(cum_col[:, h : h + 1] - cum[h : h + 1] + far) * dt
            high, low = split(scores * weight)
            x_h = xt_ref[i, part, :]
            dy_h = dyt_ref[i, part, :]
            yt_ref[i, part, :] = dot(x_h, high, NT) + dot(x_h, low, NT)
            dxt_ref[i, part, :] = dot(dy_h, high) + dot(dy_h, low)
            mine = (lanes < P_SIZE) if h == 0 else (lanes >= P_SIZE)
            mixing_grad = dot(jnp.where(mine, dy_n, jnp.zeros_like(dy_n)), x_t)
            score_grad = mixing_grad * weight if h == 0 else score_grad + mixing_grad * weight
        high, low = split(score_grad)
        dct_ref[i] = dot(b_t, high, NT) + dot(b_t, low, NT)
        dbt_ref[i] = dot(c_t, high) + dot(c_t, low)
        return carry

    lax.fori_loop(0, groups, group, 0)


def group_grad_kernel(
    ends_mine, ends_other, sums_mine, sums_other, rows_ref,
    xt_ref, dyt_ref, dct_ref, dbt_ref,
    own_ref, first1_ref, first3_ref, last1_ref, last3_ref, states_ref,
):
    groups, _, _ = xt_ref.shape
    owned = groups // 4
    me = lax.axis_index("mp")
    refs = (ends_mine, ends_other, sums_mine, sums_other)
    for k, (ref, place) in enumerate((
        (own_ref, 0), (own_ref, 2), (last1_ref, 0), (last1_ref, 2),
        (first1_ref, 0), (first3_ref, 0), (last3_ref, 0), (last3_ref, 2),
    )):
        g = lax.bitwise_xor(me, k // owned) * owned + k % owned
        for which, (at, vals_ref, weights, base_ref) in enumerate((
            (0, dyt_ref, ENTRY, dct_ref),
            (P_SIZE, xt_ref, TAIL, dbt_ref),
        )):
            total = base_ref[g]
            for h, state in enumerate(states_of(refs, g, groups, at)):
                states_ref[2 * g + h, at : at + P_SIZE] = state
                high, low = split(state)
                vals = vals_ref[g, h * P_SIZE : (h + 1) * P_SIZE, :]
                grad = dot(
                    jnp.concatenate([high, low], axis=0),
                    jnp.concatenate([vals, vals], axis=0),
                    TN,
                )
                total = total + grad * rows_ref[row_of(weights, g, h), :]
            ref[place + which] = total


def relay_kernel(part1_ref, part3_ref, got3_ref, got1_ref, out1_ref, out3_ref):
    out1_ref[...] = part1_ref[...] + got3_ref[...]
    out3_ref[...] = part3_ref[...] + got1_ref[...]


def finish_kernel(
    states_ref, rows_ref, xt_ref, dyt_ref, bt_ref, ct_ref, yt_ref, dxt_ref,
    rate_ref, gain_ref, order_ref,
    out_ref, dx_ref, raw_grad_ref, stats_ref,
    through, back, skip, bound,
):
    groups, _, length = xt_ref.shape
    pairs = 2 * groups
    both_heads = lax.broadcasted_iota(jnp.int32, (128, length), 0) < P_SIZE

    def group(g):
        x_t, dy_t = xt_ref[g].astype(F32), dyt_ref[g].astype(F32)
        states = [states_ref[2 * g + h, :P_SIZE] for h in range(2)]
        adjoints = [states_ref[2 * g + h, P_SIZE:] for h in range(2)]

        def entering(state, other):
            high, low = split(jnp.concatenate(state, axis=0))
            return dot(
                jnp.concatenate([high, low], axis=1), jnp.concatenate([other, other], axis=0)
            )

        y_t = yt_ref[g] + entering(states, ct_ref[g]) * two_heads(rows_ref, ENTRY, g, length)
        dx_far = entering(adjoints, bt_ref[g]) * two_heads(rows_ref, TAIL, g, length)
        dx_t = dxt_ref[g] + dx_far
        gain = jnp.where(both_heads, gain_ref[0, g], gain_ref[1, g])
        out_ref[g] = (y_t + gain * x_t).astype(BF16)
        dx_ref[g] = (dx_t + gain * dy_t).astype(BF16)
        forward, backward = dy_t * y_t, x_t * dx_t
        direct, far = dy_t * x_t, x_t * dx_far
        for h in range(2):
            part = slice(h * P_SIZE, (h + 1) * P_SIZE)
            at = row_of(0, g, h)
            through[at, :] = jnp.sum(forward[part], axis=0, keepdims=True)
            back[at, :] = jnp.sum(backward[part], axis=0, keepdims=True)
            skip[at, :] = jnp.sum(direct[part], axis=0, keepdims=True)
            meet = jnp.sum(states[h] * adjoints[h], axis=0, keepdims=True)
            passed = rows_ref[row_of(ENTRY, g, h), :][:, length - 1 :]
            arrive = jnp.sum(far[part], axis=0, keepdims=True)
            bound[at, :] = arrive + jnp.concatenate(
                [meet * passed, jnp.zeros((1, length - N), F32)], axis=1
            )

    for g in range(groups):
        group(g)
    dt = rows_ref[DT : DT + 16]
    rate = jnp.exp(pair_rows(rate_ref, pairs, length))
    before = lax.broadcasted_iota(jnp.int32, (length, length), 0)
    after = lax.broadcasted_iota(jnp.int32, (length, length), 1)
    since = jnp.where(before >= after, 1.0, 0.0).astype(F32)
    decay_grad = exact_dot(through[...] - back[...], since)
    decay_grad = decay_grad + jnp.sum(bound[...], axis=1, keepdims=True)
    raw_grad = (back[...] / dt - rate * decay_grad) * rows_ref[SIG : SIG + 16]
    for g in range(groups):
        raw_grad_ref[g] = jnp.concatenate(
            [raw_grad[g : g + 1], raw_grad[groups + g : groups + g + 1]], axis=0
        )
    rate_grad = jnp.sum(decay_grad * rows_ref[LOGD : LOGD + 16], axis=1, keepdims=True)
    bias_grad = jnp.sum(raw_grad, axis=1, keepdims=True)
    gain_grad = jnp.sum(skip[...], axis=1, keepdims=True)
    lane = lax.broadcasted_iota(jnp.int32, (pairs, 128), 1)
    stats = jnp.where(
        lane == 0, rate_grad, jnp.where(lane == 1, bias_grad, jnp.where(lane == 2, gain_grad, 0.0))
    )
    stats = jnp.concatenate([stats, jnp.zeros((128 - pairs, 128), F32)], axis=0).T[:8]
    for k in range(stats_ref.shape[0]):
        stats_ref[k] = stats


def outputs_kernel(out_in_ref, dx_in_ref, out_ref, dx_ref, ys, dxs):
    groups, _, length = out_in_ref.shape

    for src, dst, final in ((out_in_ref, ys, out_ref), (dx_in_ref, dxs, dx_ref)):
        for g in range(groups):
            dst[pl.ds(g, length, stride=groups), :] = src[g].astype(F32).T
        final[...] = dst[...].reshape(length, groups, 128).astype(BF16)


def gather_kernel(own_ref, last1_ref, last3_ref, key_ref, query_ref, keys, queries):
    length = own_ref.shape[2]
    for slot in range(4):
        total = own_ref[slot] + last1_ref[slot] + last3_ref[slot]
        dst = keys if slot % 2 else queries
        dst[pl.ds(slot // 2, length, stride=2), :] = total.T
    key_ref[...] = keys[...].reshape(key_ref.shape).astype(BF16)
    query_ref[...] = queries[...].reshape(query_ref.shape).astype(BF16)


def row_sum_kernel(got_ref, send_ref):
    total = got_ref[0]
    for k in range(1, got_ref.shape[0]):
        total = total + got_ref[k]
    for k in range(send_ref.shape[0]):
        send_ref[k] = total


def final_sum_kernel(got_ref, rate_ref, bias_ref, gain_ref):
    total = got_ref[0]
    for k in range(1, got_ref.shape[0]):
        total = total + got_ref[k]
    groups = rate_ref.shape[1]
    for k, ref in enumerate((rate_ref, bias_ref, gain_ref)):
        for h in range(2):
            ref[h : h + 1, :] = total[k : k + 1, h * groups : (h + 1) * groups]


def call(kernel, out, scratch=(), smem=(), hbm=(), flops=10**9, moved=4 << 20, vmem=24,
         out_specs=None, update=0):
    def run(*args):
        old = len(args) - update
        spaces = [
            pltpu.SMEM if i in smem else pl.ANY if i in hbm or i >= old else pltpu.VMEM
            for i in range(len(args))
        ]
        return pl.pallas_call(
            kernel,
            grid=(1,) if out_specs else (),
            out_shape=out,
            in_specs=[pl.BlockSpec(memory_space=space) for space in spaces],
            out_specs=out_specs
            or jax.tree.map(lambda _: pl.BlockSpec(memory_space=pltpu.VMEM), out),
            input_output_aliases={old + k: k for k in range(update)},
            scratch_shapes=list(scratch),
            cost_estimate=pl.CostEstimate(flops=flops, bytes_accessed=moved, transcendentals=0),
            compiler_params=pltpu.CompilerParams(vmem_limit_bytes=vmem << 20),
        )(*args)

    return run


def local(
    features, key_projection, query_proj, step_raw, doc_starts, log_rate, step_bias, skip_gain,
    out_grad,
):
    _, length, groups, _ = features.shape
    pairs = 2 * groups
    half = groups // 2
    shards, owners = lax.axis_size("seq"), lax.axis_size("mp")
    shape = jax.ShapeDtypeStruct
    flat = pltpu.VMEM((length * groups, 128), F32)
    per_pair = pltpu.VMEM((pairs, length), F32)
    summary = shape((groups, 2 * P_SIZE + 8, N), F32)
    entering = shape((groups, 2 * P_SIZE, N), F32)
    rate, bias, gain = log_rate.T, step_bias.T, skip_gain.T
    partner = [(i, i ^ 1) for i in range(shards)]
    cores = [list(range(c, shards, 2)) for c in range(2)]

    def to_chips(a):
        return lax.all_to_all(a, "seq", 0, 0, axis_index_groups=cores, tiled=True)

    keep, give, rows = call(
        summary_kernel,
        (summary, summary, shape((ROWS, length), F32)),
        scratch=[flat] * 4 + [pltpu.VMEM((length, groups, 128), BF16)] * 4
        + [pltpu.VMEM((groups, 2, length), F32), pltpu.VMEM((1, length), jnp.int32)]
        + [pltpu.SMEM((2, groups), F32)] * 2 + [pltpu.SemaphoreType.DMA((8,))],
        hbm=range(8), vmem=62,
    )(features[0], out_grad[0], key_projection[0], query_proj[0],
      step_raw[0].transpose(1, 2, 0), doc_starts, rate, bias)
    got = lax.ppermute(give, "seq", partner)
    chip = call(chip_kernel, summary)(keep, got)
    scanned = call(scan_kernel, entering)(to_chips(chip))
    ends = to_chips(scanned)
    ends_other = lax.ppermute(ends, "seq", partner)
    got_rest = lax.ppermute(keep, "seq", partner)
    full, wide = shape((groups, 128, length), F32), shape((groups, 128, length), BF16)
    within = ()
    for start in (0, half):
        block = pl.BlockSpec((half, 128, length), functools.partial(lambda at, _: (at, 0, 0), start // half))
        within = call(
            functools.partial(within_kernel, start), (full,) * 4 + (wide,) * 4,
            scratch=[flat] * 4, flops=10**10, vmem=60, out_specs=(block,) * 8, update=len(within),
        )(features[0], out_grad[0], key_projection[0], query_proj[0], rows, *within)
    y_in, dx_in, dc_in, db_in, x_t, dy_t, b_t, c_t = within
    owned = groups // owners
    part, half_part = shape((2 * owned, 128, length), F32), shape((owned, 128, length), F32)
    own, first1, first3, last1, last3, states = call(
        group_grad_kernel,
        (part, half_part, half_part, part, part, shape((pairs, 2 * P_SIZE, N), F32)),
        vmem=60,
    )(ends, ends_other, got, got_rest, rows, x_t, dy_t, dc_in, db_in)

    def to_neighbour(a, k):
        return lax.ppermute(a, "mp", [(i, i ^ k) for i in range(owners)])

    got1, got3 = to_neighbour(first1, 1), to_neighbour(first3, 3)
    mixed, dx, raw_grad, stats = call(
        finish_kernel,
        (wide, wide, shape((groups, 2, length), F32), shape((lax.axis_size("dp"), 8, 128), F32)),
        scratch=[per_pair, per_pair, per_pair, per_pair], smem=(8, 9), hbm=(10,), vmem=60,
    )(states, rows, x_t, dy_t, b_t, c_t, y_in, dx_in, rate, gain, own)
    stats = lax.all_to_all(stats, "dp", 0, 0, tiled=True)
    mixed, dx = call(
        outputs_kernel, (shape((length, groups, 128), BF16),) * 2, scratch=[flat, flat], vmem=24
    )(mixed, dx)
    stats = call(row_sum_kernel, shape((shards, 8, 128), F32), vmem=2)(stats)
    low = pl.BlockSpec((owned, 128, length), lambda _: (0, 0, 0))
    high = pl.BlockSpec((owned, 128, length), lambda _: (1, 0, 0))
    last1, last3 = pl.pallas_call(
        relay_kernel,
        name="relay",
        grid=(1,),
        out_shape=(part, part),
        in_specs=(high, low, low, low),
        out_specs=(high, low),
        input_output_aliases={0: 0, 1: 1},
        cost_estimate=pl.CostEstimate(flops=10**6, bytes_accessed=3 << 19, transcendentals=0),
        compiler_params=pltpu.CompilerParams(vmem_limit_bytes=60 << 20),
    )(last1, last3, got3, got1)
    last1, last3 = to_neighbour(last1, 1), to_neighbour(last3, 3)
    stats = lax.all_to_all(stats, "seq", 0, 0, tiled=True)
    sums = call(final_sum_kernel, (shape((2, groups), F32),) * 3, vmem=2)(stats)
    out_grads = shape((length, owned, 128), BF16)
    key_grad, query_grad = call(
        gather_kernel, (out_grads, out_grads),
        scratch=[pltpu.VMEM((length * owned, 128), F32)] * 2, vmem=24,
    )(own, last1, last3)
    return (
        mixed[None],
        dx[None],
        key_grad[None],
        query_grad[None],
        raw_grad.transpose(2, 0, 1)[None],
        *(total.T for total in sums),
    )


def solution(mesh):
    return jax.shard_map(
        local,
        mesh=mesh,
        in_specs=(
            P("dp", "seq", None, "mp"),
            P("dp", "seq", None, None),
            P("dp", "seq", None, None),
            P("dp", "seq", None, "mp"),
            P("dp", "seq"),
            P(None, "mp"),
            P(None, "mp"),
            P(None, "mp"),
            P("dp", "seq", None, "mp"),
        ),
        out_specs=(
            P("dp", "seq", None, "mp"),
            P("dp", "seq", None, "mp"),
            P("dp", "seq", "mp", None),
            P("dp", "seq", "mp", None),
            P("dp", "seq", None, "mp"),
            P(None, "mp"),
            P(None, "mp"),
            P(None, "mp"),
        ),
        check_vma=False,
    )
```

profile of v0, /device:TPU:6, one launch (start us, length us, event | category | flops | bytes accessed | tf_op | source)
XLA Modules:
  0.0 132.9 jit_solution(7925639738957099834)
XLA Ops:
  0.6 3.9 %shard_map.152 = (f32[8,136,128]{2,1,0:T(8,128)}, f32[8,136,128]{2,1,0:T(8,128)}, f32[104,256]{1,0:T(8,128)}) custom-call(bf16[256,8,128]{2,1,0:T(8,128)(2,1)} %bitcast.23, bf16[256,8,128]{2,1,0:T(8,128)(2,1)} %bitcast.26, bf16[256,8,128]{2,1,0:T(8,128)(2,1)} %bitcast.29, bf16[256,8,128]{2,1,0:T(8,128)(2,1)} %bitcast.32, f32[8,2,256]{2,1,0:T(2,128)} %bitcast.35, ...), custom_call_target="tpu_custom_call" | custom-call | flops 1000000000 | bytes 4194304 | tf_op jit(solution)/shard_map/pallas_call | solution.py:402
  4.5 1.9 %collective-permute-start = (f32[8,136,128]{2,1,0:T(8,128)}, f32[8,136,128]{2,1,0:T(8,128)S(1)}, u32[]{:S(2)}, u32[]{:S(2)}) collective-permute-start(f32[8,136,128]{2,1,0:T(8,128)} %get-tuple-element.47), channel_id=1, source_target_pairs={{0,32},{32,0},{64,96},{96,64},{128,160},{160,128},{192,224},{224,1... | collective-permute-start | bytes 1671176 | tf_op jit(solution)/shard_map/ppermute | solution.py:447
  6.5 2.1 %collective-permute-done.got_ref.sums_mine = f32[8,136,128]{2,1,0:T(8,128)S(1)} collective-permute-done((f32[8,136,128]{2,1,0:T(8,128)}, f32[8,136,128]{2,1,0:T(8,128)S(1)}, u32[]{:S(2)}, u32[]{:S(2)}) %collective-permute-start) | collective-permute-done | bytes 557088 | tf_op jit(solution)/shard_map/ppermute | solution.py:447
  8.6 1.3 copy-done.2
  9.9 0.9 shard_map.153
  10.8 10.4 %all-to-all-start = ((f32[8,136,128]{2,1,0:T(8,128)}), f32[8,136,128]{2,1,0:T(8,128)S(1)}, u32[]{:S(2)}, u32[]{:S(2)}) async-start(f32[8,136,128]{2,1,0:T(8,128)} %shard_map.153), calls=%async_computation | async-start | bytes 1114112 | tf_op jit(solution)/shard_map/all_to_all | solution.py:436
  21.2 1.9 %collective-permute-start.2 = (f32[8,136,128]{2,1,0:T(8,128)S(1)}, f32[8,136,128]{2,1,0:T(8,128)S(1)}, u32[]{:S(2)}, u32[]{:S(2)}) collective-permute-start(f32[8,136,128]{2,1,0:T(8,128)S(1)} %copy-done.3), channel_id=1, source_target_pairs={{0,32},{32,0},{64,96},{96,64},{128,160},{160,128},{192,224},{224,1... | collective-permute-start | bytes 1671176 | tf_op jit(solution)/shard_map/ppermute | solution.py:452
  23.1 16.6 %all-to-all-done.recv_ref = f32[8,136,128]{2,1,0:T(8,128)S(1)} async-done(((f32[8,136,128]{2,1,0:T(8,128)}), f32[8,136,128]{2,1,0:T(8,128)S(1)}, u32[]{:S(2)}, u32[]{:S(2)}) %all-to-all-start) | async-done | bytes 557088 | tf_op jit(solution)/shard_map/all_to_all | solution.py:436
  39.7 0.8 shard_map.154
  40.5 3.5 %all-to-all-start.1 = ((f32[8,128,128]{2,1,0:T(8,128)}), f32[8,128,128]{2,1,0:T(8,128)S(1)}, u32[]{:S(2)}, u32[]{:S(2)}) async-start(f32[8,128,128]{2,1,0:T(8,128)} %shard_map.154), calls=%async_computation.1 | async-start | bytes 1048576 | tf_op jit(solution)/shard_map/all_to_all | solution.py:436
  44.0 7.2 %shard_map.155 = (f32[8,128,256]{2,1,0:T(8,128)}, f32[8,128,256]{2,1,0:T(8,128)}, f32[8,128,256]{2,1,0:T(8,128)}, f32[8,128,256]{2,1,0:T(8,128)}, bf16[8,128,256...) custom-call(bf16[256,8,128]{2,1,0:T(8,128)(2,1)} %bitcast.24, ...), custom_call_target="tpu_custom_call" | custom-call | flops 10000000000 | bytes 4194304 | tf_op jit(solution)/shard_map/pallas_call | solution.py:402
  51.2 10.7 %all-to-all-done.1.ends_mine = f32[8,128,128]{2,1,0:T(8,128)S(1)} async-done(((f32[8,128,128]{2,1,0:T(8,128)}), f32[8,128,128]{2,1,0:T(8,128)S(1)}, u32[]{:S(2)}, u32[]{:S(2)}) %all-to-all-start.1) | async-done | bytes 524320 | tf_op jit(solution)/shard_map/all_to_all | solution.py:436
  61.9 1.9 %collective-permute-start.1 = (f32[8,128,128]{2,1,0:T(8,128)S(1)}, f32[8,128,128]{2,1,0:T(8,128)S(1)}, u32[]{:S(2)}, u32[]{:S(2)}) collective-permute-start(f32[8,128,128]{2,1,0:T(8,128)S(1)} %all-to-all-done.1.ends_mine), channel_id=1, source_target_pairs={{0,32},{32,0},{64,96},{96,64},{128,160},{160,128},{192,224},{224,1... | collective-permute-start | bytes 1572872 | tf_op jit(solution)/shard_map/ppermute | solution.py:451
  63.8 7.3 %shard_map.156 = (f32[8,128,256]{2,1,0:T(8,128)}, f32[8,128,256]{2,1,0:T(8,128)}, f32[8,128,256]{2,1,0:T(8,128)}, f32[8,128,256]{2,1,0:T(8,128)}, bf16[8,128,256...) custom-call(bf16[256,8,128]{2,1,0:T(8,128)(2,1)} %bitcast.25, ...), custom_call_target="tpu_custom_call", output_to_operand_aliasing={{0}: (5, {}), {1}: (6, {}), {2}: (7, {}), {3}: (8, {}), {4}... | custom-call | flops 10000000000 | bytes 4194304 | tf_op jit(solution)/shard_map/pallas_call | solution.py:402
  71.2 0.8 copy-done.7
  72.1 5.0 %shard_map.157 = (f32[4,128,256]{2,1,0:T(8,128)}, f32[2,128,256]{2,1,0:T(8,128)}, f32[2,128,256]{2,1,0:T(8,128)}, f32[4,128,256]{2,1,0:T(8,128)}, f32[4,128,256]{2,1,0:T(8,128)}, /*index=5*/f32[16,128,128]{2,1,0:T(8,128)}) custom-call(f32[8,128,128]{2,1,0:T(8,128)} %copy-done.6, f32[8,128,128]{2,1,0:T(8,128)} %copy-done.8, f32[8,136,128]{2,1,0:T(8,128)} %copy-done, ...), custom_call_target="tpu_custom_call" | custom-call | flops 1000000000 | bytes 4194304 | tf_op jit(solution)/shard_map/pallas_call | solution.py:402
  77.1 2.4 %collective-permute-start.3 = (f32[2,128,256]{2,1,0:T(8,128)}, f32[2,128,256]{2,1,0:T(8,128)S(1)}, u32[]{:S(2)}, u32[]{:S(2)}) collective-permute-start(f32[2,128,256]{2,1,0:T(8,128)} %get-tuple-element.73), channel_id=1, source_target_pairs={{0,3},{1,2},{2,1},{3,0},{4,7},{5,6},{6,5},{7,4},{8,11},{9,10},{10,... | collective-permute-start | bytes 786440 | tf_op jit(solution)/shard_map/ppermute | solution.py:471
  79.5 2.8 %collective-permute-start.4 = (f32[2,128,256]{2,1,0:T(8,128)}, f32[2,128,256]{2,1,0:T(8,128)S(1)}, u32[]{:S(2)}, u32[]{:S(2)}) collective-permute-start(f32[2,128,256]{2,1,0:T(8,128)} %get-tuple-element.74), channel_id=1, source_target_pairs={{0,1},{1,0},{2,3},{3,2},{4,5},{5,4},{6,7},{7,6},{8,9},{9,8},{10,11... | collective-permute-start | bytes 786440 | tf_op jit(solution)/shard_map/ppermute | solution.py:471
  82.3 6.8 %collective-permute-done.3.got3_ref = f32[2,128,256]{2,1,0:T(8,128)S(1)} collective-permute-done((f32[2,128,256]{2,1,0:T(8,128)}, f32[2,128,256]{2,1,0:T(8,128)S(1)}, u32[]{:S(2)}, u32[]{:S(2)}) %collective-permute-start.3) | collective-permute-done | bytes 262176 | tf_op jit(solution)/shard_map/ppermute | solution.py:471
  89.1 0.9 collective-permute-done.4.got1_ref
  90.0 0.7 copy-done.10
  90.7 2.0 %relay.1 = (f32[4,128,256]{2,1,0:T(8,128)}, f32[4,128,256]{2,1,0:T(8,128)}) custom-call(f32[4,128,256]{2,1,0:T(8,128)} %get-tuple-element.71.part1_ref, f32[4,128,256]{2,1,0:T(8,128)} %get-tuple-element.72.part3_ref, f32[2,128,256]{2,1,0:T(8,128)} %copy-done.9, f32[2,128,256]{2,1,0:T(8,128)} %copy-done.10), custom_call_target="tpu_custom_call", output_to_operand_aliasing={{0}: (0, {}), {1}: (1, {})} | custom-call | flops 1000000 | bytes 1572864 | tf_op jit(solution)/shard_map/relay/pallas_call | solution.py:486
  92.7 2.8 %collective-permute-start.5 = (f32[4,128,256]{2,1,0:T(8,128)}, f32[4,128,256]{2,1,0:T(8,128)S(1)}, u32[]{:S(2)}, u32[]{:S(2)}) collective-permute-start(f32[4,128,256]{2,1,0:T(8,128)} %get-tuple-element.75), channel_id=1, source_target_pairs={{0,1},{1,0},{2,3},{3,2},{4,5},{5,4},{6,7},{7,6},{8,9},{9,8},{10,11... | collective-permute-start | bytes 1572872 | tf_op jit(solution)/shard_map/ppermute | solution.py:471
  95.5 4.1 %collective-permute-start.6 = (f32[4,128,256]{2,1,0:T(8,128)}, f32[4,128,256]{2,1,0:T(8,128)S(1)}, u32[]{:S(2)}, u32[]{:S(2)}) collective-permute-start(f32[4,128,256]{2,1,0:T(8,128)} %get-tuple-element.76), channel_id=1, source_target_pairs={{0,3},{1,2},{2,1},{3,0},{4,7},{5,6},{6,5},{7,4},{8,11},{9,10},{10,... | collective-permute-start | bytes 1572872 | tf_op jit(solution)/shard_map/ppermute | solution.py:471
  99.6 4.6 %shard_map.158 = (bf16[8,128,256]{2,1,0:T(8,128)(2,1)}, bf16[8,128,256]{2,1,0:T(8,128)(2,1)}, f32[8,2,256]{2,1,0:T(2,128)}, f32[8,8,128]{2,1,0:T(8,128)}) custom-call(f32[16,128,128]{2,1,0:T(8,128)} %get-tuple-element.61.states_ref, f32[104,256]{1,0:T(8,128)} %get-tuple-element.48.rows_ref, bf16[8,128,256]{2,1,0:T(8,128)(2,1)} %get-tuple-element.57.xt_ref, ...), custom_call_target="tpu_custom_call" | custom-call | flops 1000000000 | bytes 4194304 | tf_op jit(solution)/shard_map/pallas_call | solution.py:402
  104.2 15.1 %all_to_all.20.got_ref = f32[8,8,128]{2,1,0:T(8,128)S(1)} all-to-all(f32[8,8,128]{2,1,0:T(8,128)} %get-tuple-element.80), channel_id=1, replica_groups=mesh['seq'=16,'dp'=8,'mp'=4] {'dp'}, dimensions={0} | all-to-all | bytes 65536 | tf_op jit(solution)/shard_map/all_to_all | solution.py:479
  119.3 0.6 shard_map.161
  119.9 3.5 %all-to-all-start.3 = ((f32[16,8,128]{2,1,0:T(8,128)}), f32[16,8,128]{2,1,0:T(8,128)S(1)}, u32[]{:S(2)}, u32[]{:S(2)}) async-start(f32[16,8,128]{2,1,0:T(8,128)} %shard_map.161), calls=%async_computation.3 | async-start | bytes 131072 | tf_op jit(solution)/shard_map/all_to_all | solution.py:498
  123.5 1.4 %shard_map.159 = (bf16[256,8,128]{2,1,0:T(8,128)(2,1)}, bf16[256,8,128]{2,1,0:T(8,128)(2,1)}) custom-call(bf16[8,128,256]{2,1,0:T(8,128)(2,1)S(1)} %copy-done.4, bf16[8,128,256]{2,1,0:T(8,128)(2,1)S(1)} %copy-done.5), custom_call_target="tpu_custom_call" | custom-call | flops 1000000000 | bytes 4194304 | tf_op jit(solution)/shard_map/pallas_call | solution.py:402
  124.8 6.4 %all-to-all-done.3.got_ref = f32[16,8,128]{2,1,0:T(8,128)S(1)} async-done(((f32[16,8,128]{2,1,0:T(8,128)}), f32[16,8,128]{2,1,0:T(8,128)S(1)}, u32[]{:S(2)}, u32[]{:S(2)}) %all-to-all-start.3) | async-done | bytes 65568 | tf_op jit(solution)/shard_map/all_to_all | solution.py:498
  131.2 0.7 shard_map.162
  131.9 1.0 shard_map.160
  (23 shorter events, 0.2 us)
Async XLA Ops:
  4.5 4.1 %collective-permute-start = (f32[8,136,128]{2,1,0:T(8,128)}, f32[8,136,128]{2,1,0:T(8,128)S(1)}, u32[]{:S(2)}, u32[]{:S(2)}) collective-permute-start(f32[8,136,128]{2,1,0:T(8,128)} %get-tuple-element.47), channel_id=1, source_target_pairs={{0,32},{32,0},{64,96},{96,64},{128,160},{160,128},{192,224},{224,1... | collective-permute-start | bytes 1671176 | tf_op jit(solution)/shard_map/ppermute | solution.py:447
  8.6 2.1 %copy-start = (f32[8,136,128]{2,1,0:T(8,128)}, f32[8,136,128]{2,1,0:T(8,128)S(1)}, u32[]{:S(2)}) copy-start(f32[8,136,128]{2,1,0:T(8,128)S(1)} %collective-permute-done.got_ref.sums_mine) | copy-start | bytes 1671172
  8.6 1.3 copy-start.2
  10.8 10.5 %copy-start.3 = (f32[8,136,128]{2,1,0:T(8,128)S(1)}, f32[8,136,128]{2,1,0:T(8,128)}, u32[]{:S(2)}) copy-start(f32[8,136,128]{2,1,0:T(8,128)} %get-tuple-element.46.keep_ref) | copy-start | bytes 1671172
  10.8 28.9 %all-to-all-start = ((f32[8,136,128]{2,1,0:T(8,128)}), f32[8,136,128]{2,1,0:T(8,128)S(1)}, u32[]{:S(2)}, u32[]{:S(2)}) async-start(f32[8,136,128]{2,1,0:T(8,128)} %shard_map.153), calls=%async_computation | async-start | bytes 1114112 | tf_op jit(solution)/shard_map/all_to_all | solution.py:436
  21.2 49.9 %collective-permute-start.2 = (f32[8,136,128]{2,1,0:T(8,128)S(1)}, f32[8,136,128]{2,1,0:T(8,128)S(1)}, u32[]{:S(2)}, u32[]{:S(2)}) collective-permute-start(f32[8,136,128]{2,1,0:T(8,128)S(1)} %copy-done.3), channel_id=1, source_target_pairs={{0,32},{32,0},{64,96},{96,64},{128,160},{160,128},{192,224},{224,1... | collective-permute-start | bytes 1671176 | tf_op jit(solution)/shard_map/ppermute | solution.py:452
  40.5 21.4 %all-to-all-start.1 = ((f32[8,128,128]{2,1,0:T(8,128)}), f32[8,128,128]{2,1,0:T(8,128)S(1)}, u32[]{:S(2)}, u32[]{:S(2)}) async-start(f32[8,128,128]{2,1,0:T(8,128)} %shard_map.154), calls=%async_computation.1 | async-start | bytes 1048576 | tf_op jit(solution)/shard_map/all_to_all | solution.py:436
  61.9 9.2 %copy-start.6 = (f32[8,128,128]{2,1,0:T(8,128)}, f32[8,128,128]{2,1,0:T(8,128)S(1)}, u32[]{:S(2)}) copy-start(f32[8,128,128]{2,1,0:T(8,128)S(1)} %all-to-all-done.1.ends_mine) | copy-start | bytes 1572868
  61.9 9.2 %collective-permute-start.1 = (f32[8,128,128]{2,1,0:T(8,128)S(1)}, f32[8,128,128]{2,1,0:T(8,128)S(1)}, u32[]{:S(2)}, u32[]{:S(2)}) collective-permute-start(f32[8,128,128]{2,1,0:T(8,128)S(1)} %all-to-all-done.1.ends_mine), channel_id=1, source_target_pairs={{0,32},{32,0},{64,96},{96,64},{128,160},{160,128},{192,224},{224,1... | collective-permute-start | bytes 1572872 | tf_op jit(solution)/shard_map/ppermute | solution.py:451
  71.1 0.8 copy-start.7
  71.1 1.0 copy-start.8
  77.1 12.0 %collective-permute-start.3 = (f32[2,128,256]{2,1,0:T(8,128)}, f32[2,128,256]{2,1,0:T(8,128)S(1)}, u32[]{:S(2)}, u32[]{:S(2)}) collective-permute-start(f32[2,128,256]{2,1,0:T(8,128)} %get-tuple-element.73), channel_id=1, source_target_pairs={{0,3},{1,2},{2,1},{3,0},{4,7},{5,6},{6,5},{7,4},{8,11},{9,10},{10,... | collective-permute-start | bytes 786440 | tf_op jit(solution)/shard_map/ppermute | solution.py:471
  79.5 10.5 %collective-permute-start.4 = (f32[2,128,256]{2,1,0:T(8,128)}, f32[2,128,256]{2,1,0:T(8,128)S(1)}, u32[]{:S(2)}, u32[]{:S(2)}) collective-permute-start(f32[2,128,256]{2,1,0:T(8,128)} %get-tuple-element.74), channel_id=1, source_target_pairs={{0,1},{1,0},{2,3},{3,2},{4,5},{5,4},{6,7},{7,6},{8,9},{9,8},{10,11... | collective-permute-start | bytes 786440 | tf_op jit(solution)/shard_map/ppermute | solution.py:471
  89.1 0.9 copy-start.9
  90.0 0.7 copy-start.10
  92.7 39.2 %collective-permute-start.5 = (f32[4,128,256]{2,1,0:T(8,128)}, f32[4,128,256]{2,1,0:T(8,128)S(1)}, u32[]{:S(2)}, u32[]{:S(2)}) collective-permute-start(f32[4,128,256]{2,1,0:T(8,128)} %get-tuple-element.75), channel_id=1, source_target_pairs={{0,1},{1,0},{2,3},{3,2},{4,5},{5,4},{6,7},{7,6},{8,9},{9,8},{10,11... | collective-permute-start | bytes 1572872 | tf_op jit(solution)/shard_map/ppermute | solution.py:471
  95.5 36.4 %collective-permute-start.6 = (f32[4,128,256]{2,1,0:T(8,128)}, f32[4,128,256]{2,1,0:T(8,128)S(1)}, u32[]{:S(2)}, u32[]{:S(2)}) collective-permute-start(f32[4,128,256]{2,1,0:T(8,128)} %get-tuple-element.76), channel_id=1, source_target_pairs={{0,3},{1,2},{2,1},{3,0},{4,7},{5,6},{6,5},{7,4},{8,11},{9,10},{10,... | collective-permute-start | bytes 1572872 | tf_op jit(solution)/shard_map/ppermute | solution.py:471
  119.3 4.2 %copy-start.4 = (bf16[8,128,256]{2,1,0:T(8,128)(2,1)S(1)}, bf16[8,128,256]{2,1,0:T(8,128)(2,1)}, u32[]{:S(2)}) copy-start(bf16[8,128,256]{2,1,0:T(8,128)(2,1)} %get-tuple-element.67.out_in_ref) | copy-start | bytes 1572868
  119.3 4.2 %copy-start.5 = (bf16[8,128,256]{2,1,0:T(8,128)(2,1)S(1)}, bf16[8,128,256]{2,1,0:T(8,128)(2,1)}, u32[]{:S(2)}) copy-start(bf16[8,128,256]{2,1,0:T(8,128)(2,1)} %get-tuple-element.68.dx_in_ref) | copy-start | bytes 1572868
  119.9 11.3 %all-to-all-start.3 = ((f32[16,8,128]{2,1,0:T(8,128)}), f32[16,8,128]{2,1,0:T(8,128)S(1)}, u32[]{:S(2)}, u32[]{:S(2)}) async-start(f32[16,8,128]{2,1,0:T(8,128)} %shard_map.161), calls=%async_computation.3 | async-start | bytes 131072 | tf_op jit(solution)/shard_map/all_to_all | solution.py:498
  124.8 7.0 %copy-start.1 = (f32[4,128,256]{2,1,0:T(8,128)S(1)}, f32[4,128,256]{2,1,0:T(8,128)}, u32[]{:S(2)}) copy-start(f32[4,128,256]{2,1,0:T(8,128)} %get-tuple-element.66.order_ref.own_ref) | copy-start | bytes 1572868
where the time goes:
time: 136 us; the launch traced here: 133 us
  waiting for transfers between devices  43.5 us (32%)
  Pallas kernels  35.3 us (26%)
  starting transfers between devices  35.2 us (26%)
  blocking collectives  15.1 us (11%)
  local copies, waits for them, and re-layouts  2.93 us (2%)
    pallas_call x11, Pallas kernels, run(): pl.pallas_call(kernel, grid=(1,) if out_specs else (), out_shape=out, in_...  33.3 us
    all_to_all x2, waiting for transfers between devices, to_chips(): return lax.all_to_all(a, 'seq', 0, 0, axis_index_groups=cores, tiled=True)  27.2 us
    all_to_all x1, blocking collectives, local(): stats = lax.all_to_all(stats, 'dp', 0, 0, tiled=True)  15.1 us
    all_to_all x2, starting transfers between devices, to_chips(): return lax.all_to_all(a, 'seq', 0, 0, axis_index_groups=cores, tiled=True)  13.9 us
    ppermute x4, starting transfers between devices, to_neighbour(): return lax.ppermute(a, 'mp', [(i, i ^ k) for i in range(owners)])  12 us
    ppermute x4, waiting for transfers between devices, to_neighbour(): return lax.ppermute(a, 'mp', [(i, i ^ k) for i in range(owners)])  7.72 us
    all_to_all x1, waiting for transfers between devices, local(): stats = lax.all_to_all(stats, 'seq', 0, 0, tiled=True)  6.38 us
    all_to_all x1, starting transfers between devices, local(): stats = lax.all_to_all(stats, 'seq', 0, 0, tiled=True)  3.5 us
  transfers between devices with their start and end apart: 10, of which 6 were waited for; matrix products, arithmetic and copies ran while one was open for 0% of the time, Pallas kernels for 17%

commit v1 on v0

--- a/solution.py
+++ b/solution.py
@@ -464,7 +464,7 @@
     own, first1, first3, last1, last3, states = call(
         group_grad_kernel,
         (part, half_part, half_part, part, part, shape((pairs, 2 * P_SIZE, N), F32)),
-        vmem=60,
+        vmem=48,
     )(ends, ends_other, got, got_rest, rows, x_t, dy_t, dc_in, db_in)
 
     def to_neighbour(a, k):
@@ -473,14 +473,14 @@
     got1, got3 = to_neighbour(first1, 1), to_neighbour(first3, 3)
     mixed, dx, raw_grad, stats = call(
         finish_kernel,
-        (wide, wide, shape((groups, 2, length), F32), shape((lax.axis_size("dp"), 8, 128), F32)),
-        scratch=[per_pair, per_pair, per_pair, per_pair], smem=(8, 9), hbm=(10,), vmem=60,
+        (wide, wide, shape((groups, 2, length), F32), shape((shards, 8, 128), F32)),
+        scratch=[per_pair, per_pair, per_pair, per_pair], smem=(8, 9), hbm=(10,), vmem=28,
     )(states, rows, x_t, dy_t, b_t, c_t, y_in, dx_in, rate, gain, own)
-    stats = lax.all_to_all(stats, "dp", 0, 0, tiled=True)
+    stats = lax.all_to_all(stats, "seq", 0, 0, tiled=True)
     mixed, dx = call(
         outputs_kernel, (shape((length, groups, 128), BF16),) * 2, scratch=[flat, flat], vmem=24
     )(mixed, dx)
-    stats = call(row_sum_kernel, shape((shards, 8, 128), F32), vmem=2)(stats)
+    stats = call(row_sum_kernel, shape((lax.axis_size("dp"), 8, 128), F32), vmem=2)(stats)
     low = pl.BlockSpec((owned, 128, length), lambda _: (0, 0, 0))
     high = pl.BlockSpec((owned, 128, length), lambda _: (1, 0, 0))
     last1, last3 = pl.pallas_call(
@@ -492,10 +492,10 @@
         out_specs=(high, low),
         input_output_aliases={0: 0, 1: 1},
         cost_estimate=pl.CostEstimate(flops=10**6, bytes_accessed=3 << 19, transcendentals=0),
-        compiler_params=pltpu.CompilerParams(vmem_limit_bytes=60 << 20),
+        compiler_params=pltpu.CompilerParams(vmem_limit_bytes=24 << 20),
     )(last1, last3, got3, got1)
     last1, last3 = to_neighbour(last1, 1), to_neighbour(last3, 3)
-    stats = lax.all_to_all(stats, "seq", 0, 0, tiled=True)
+    stats = lax.all_to_all(stats, "dp", 0, 0, tiled=True)
     sums = call(final_sum_kernel, (shape((2, groups), F32),) * 3, vmem=2)(stats)
     out_grads = shape((length, owned, 128), BF16)
     key_grad, query_grad = call(

time: 136 us -> 130 us (0.956)
  Pallas kernels: 35.3 us -> 29.8 us
  blocking collectives: 15.1 us -> 10.4 us
  starting transfers between devices: 35.2 us -> 39.1 us
  local copies, waits for them, and re-layouts: 2.93 us -> 5.61 us
    all_to_all x1, blocking collectives: 15.1 us -> 10.4 us  [local(): stats = lax.all_to_all(stats, 'seq', 0, 0, tiled=True)]
    pallas_call x11, Pallas kernels: 33.3 us -> 29.7 us  [run(): pl.pallas_call(kernel, grid=(1,) if out_specs else (), out_shape=out, in_...]
    all_to_all x1, starting transfers between devices: 3.5 us -> 7.1 us  [local(): stats = lax.all_to_all(stats, 'dp', 0, 0, tiled=True)]
    unnamed x22 -> x28, local copies, waits for them, and re-layouts: 2.93 us -> 5.61 us
    pallas_call x1, Pallas kernels: 2.01 us -> 0.09 us  [local(): pl.pallas_call(relay_kernel, name='relay', grid=(1,), out_shape=(part, pa...]
  transfers between devices with their start and end apart: 10 -> 10, of which waited for: 6 -> 6; matrix products, arithmetic and copies ran while one was open for 0% -> 0% of each run, Pallas kernels for 17% -> 16%
where the time goes in v1:
time: 130 us; the launch traced here: 128 us
  waiting for transfers between devices  42.5 us (33%)
  starting transfers between devices  39.1 us (30%)
  Pallas kernels  29.8 us (23%)
  blocking collectives  10.4 us (8%)
  local copies, waits for them, and re-layouts  5.61 us (4%)
    pallas_call x11, Pallas kernels, run(): pl.pallas_call(kernel, grid=(1,) if out_specs else (), out_shape=out, in_...  29.7 us
    all_to_all x2, waiting for transfers between devices, to_chips(): return lax.all_to_all(a, 'seq', 0, 0, axis_index_groups=cores, tiled=True)  27.3 us
    all_to_all x2, starting transfers between devices, to_chips(): return lax.all_to_all(a, 'seq', 0, 0, axis_index_groups=cores, tiled=True)  13.9 us
    ppermute x4, starting transfers between devices, to_neighbour(): return lax.ppermute(a, 'mp', [(i, i ^ k) for i in range(owners)])  12.3 us
    all_to_all x1, blocking collectives, local(): stats = lax.all_to_all(stats, 'seq', 0, 0, tiled=True)  10.4 us
    ppermute x4, waiting for transfers between devices, to_neighbour(): return lax.ppermute(a, 'mp', [(i, i ^ k) for i in range(owners)])  7.51 us
    all_to_all x1, starting transfers between devices, local(): stats = lax.all_to_all(stats, 'dp', 0, 0, tiled=True)  7.1 us
    all_to_all x1, waiting for transfers between devices, local(): stats = lax.all_to_all(stats, 'dp', 0, 0, tiled=True)  5.62 us
  transfers between devices with their start and end apart: 10, of which 6 were waited for; matrix products, arithmetic and copies ran while one was open for 0% of the time, Pallas kernels for 16%

profile of v1, /device:TPU:6, one launch (start us, length us, event | category | flops | bytes accessed | tf_op | source)
XLA Modules:
  0.0 128.2 jit_solution(14169622709147176514)
XLA Ops:
  0.6 3.9 %shard_map.152 = (f32[8,136,128]{2,1,0:T(8,128)}, f32[8,136,128]{2,1,0:T(8,128)}, f32[104,256]{1,0:T(8,128)}) custom-call(bf16[256,8,128]{2,1,0:T(8,128)(2,1)} %bitcast.23, bf16[256,8,128]{2,1,0:T(8,128)(2,1)} %bitcast.26, bf16[256,8,128]{2,1,0:T(8,128)(2,1)} %bitcast.29, bf16[256,8,128]{2,1,0:T(8,128)(2,1)} %bitcast.32, f32[8,2,256]{2,1,0:T(2,128)} %bitcast.35, ...), custom_call_target="tpu_custom_call" | custom-call | flops 1000000000 | bytes 4194304 | tf_op jit(solution)/shard_map/pallas_call | solution.py:402
  4.5 1.9 %collective-permute-start = (f32[8,136,128]{2,1,0:T(8,128)}, f32[8,136,128]{2,1,0:T(8,128)S(1)}, u32[]{:S(2)}, u32[]{:S(2)}) collective-permute-start(f32[8,136,128]{2,1,0:T(8,128)} %get-tuple-element.47), channel_id=1, source_target_pairs={{0,32},{32,0},{64,96},{96,64},{128,160},{160,128},{192,224},{224,1... | collective-permute-start | bytes 1671176 | tf_op jit(solution)/shard_map/ppermute | solution.py:447
  6.5 2.1 %collective-permute-done.got_ref.sums_mine = f32[8,136,128]{2,1,0:T(8,128)S(1)} collective-permute-done((f32[8,136,128]{2,1,0:T(8,128)}, f32[8,136,128]{2,1,0:T(8,128)S(1)}, u32[]{:S(2)}, u32[]{:S(2)}) %collective-permute-start) | collective-permute-done | bytes 557088 | tf_op jit(solution)/shard_map/ppermute | solution.py:447
  8.6 1.1 copy-done.10
  9.6 0.9 shard_map.153
  10.5 10.4 %all-to-all-start = ((f32[8,136,128]{2,1,0:T(8,128)}), f32[8,136,128]{2,1,0:T(8,128)S(1)}, u32[]{:S(2)}, u32[]{:S(2)}) async-start(f32[8,136,128]{2,1,0:T(8,128)} %shard_map.153), calls=%async_computation | async-start | bytes 1114112 | tf_op jit(solution)/shard_map/all_to_all | solution.py:436
  21.0 1.9 %collective-permute-start.2 = (f32[8,136,128]{2,1,0:T(8,128)S(1)}, f32[8,136,128]{2,1,0:T(8,128)S(1)}, u32[]{:S(2)}, u32[]{:S(2)}) collective-permute-start(f32[8,136,128]{2,1,0:T(8,128)S(1)} %copy-done.11), channel_id=1, source_target_pairs={{0,32},{32,0},{64,96},{96,64},{128,160},{160,128},{192,224},{224,1... | collective-permute-start | bytes 1671176 | tf_op jit(solution)/shard_map/ppermute | solution.py:452
  22.9 16.6 %all-to-all-done.recv_ref = f32[8,136,128]{2,1,0:T(8,128)S(1)} async-done(((f32[8,136,128]{2,1,0:T(8,128)}), f32[8,136,128]{2,1,0:T(8,128)S(1)}, u32[]{:S(2)}, u32[]{:S(2)}) %all-to-all-start) | async-done | bytes 557088 | tf_op jit(solution)/shard_map/all_to_all | solution.py:436
  39.5 0.8 shard_map.154
  40.3 3.5 %all-to-all-start.1 = ((f32[8,128,128]{2,1,0:T(8,128)}), f32[8,128,128]{2,1,0:T(8,128)S(1)}, u32[]{:S(2)}, u32[]{:S(2)}) async-start(f32[8,128,128]{2,1,0:T(8,128)} %shard_map.154), calls=%async_computation.1 | async-start | bytes 1048576 | tf_op jit(solution)/shard_map/all_to_all | solution.py:436
  43.8 7.2 %shard_map.155 = (f32[8,128,256]{2,1,0:T(8,128)}, f32[8,128,256]{2,1,0:T(8,128)}, f32[8,128,256]{2,1,0:T(8,128)}, f32[8,128,256]{2,1,0:T(8,128)}, bf16[8,128,256...) custom-call(bf16[256,8,128]{2,1,0:T(8,128)(2,1)} %bitcast.24, ...), custom_call_target="tpu_custom_call" | custom-call | flops 10000000000 | bytes 4194304 | tf_op jit(solution)/shard_map/pallas_call | solution.py:402
  51.0 10.7 %all-to-all-done.1.ends_mine = f32[8,128,128]{2,1,0:T(8,128)S(1)} async-done(((f32[8,128,128]{2,1,0:T(8,128)}), f32[8,128,128]{2,1,0:T(8,128)S(1)}, u32[]{:S(2)}, u32[]{:S(2)}) %all-to-all-start.1) | async-done | bytes 524320 | tf_op jit(solution)/shard_map/all_to_all | solution.py:436
  61.7 1.9 %collective-permute-start.1 = (f32[8,128,128]{2,1,0:T(8,128)S(1)}, f32[8,128,128]{2,1,0:T(8,128)S(1)}, u32[]{:S(2)}, u32[]{:S(2)}) collective-permute-start(f32[8,128,128]{2,1,0:T(8,128)S(1)} %all-to-all-done.1.ends_mine), channel_id=1, source_target_pairs={{0,32},{32,0},{64,96},{96,64},{128,160},{160,128},{192,224},{224,1... | collective-permute-start | bytes 1572872 | tf_op jit(solution)/shard_map/ppermute | solution.py:451
  63.6 7.3 %shard_map.156 = (f32[8,128,256]{2,1,0:T(8,128)}, f32[8,128,256]{2,1,0:T(8,128)}, f32[8,128,256]{2,1,0:T(8,128)}, f32[8,128,256]{2,1,0:T(8,128)}, bf16[8,128,256...) custom-call(bf16[256,8,128]{2,1,0:T(8,128)(2,1)} %bitcast.25, ...), custom_call_target="tpu_custom_call", output_to_operand_aliasing={{0}: (5, {}), {1}: (6, {}), {2}: (7, {}), {3}: (8, {}), {4}... | custom-call | flops 10000000000 | bytes 4194304 | tf_op jit(solution)/shard_map/pallas_call | solution.py:402
  70.9 1.0 copy-done
  72.0 1.0 copy-done.1
  73.0 3.5 %shard_map.157 = (f32[4,128,256]{2,1,0:T(8,128)S(1)}, f32[2,128,256]{2,1,0:T(8,128)S(1)}, f32[2,128,256]{2,1,0:T(8,128)S(1)}, f32[4,128,256]{2,1,0:T(8,128)S(1)}...) custom-call(f32[8,128,128]{2,1,0:T(8,128)S(1)} %all-to-all-done.1.ends_mine, ...), custom_call_target="tpu_custom_call" | custom-call | flops 1000000000 | bytes 4194304 | tf_op jit(solution)/shard_map/pallas_call | solution.py:402
  76.5 2.5 %collective-permute-start.3 = (f32[2,128,256]{2,1,0:T(8,128)S(1)}, f32[2,128,256]{2,1,0:T(8,128)S(1)}, u32[]{:S(2)}, u32[]{:S(2)}) collective-permute-start(f32[2,128,256]{2,1,0:T(8,128)S(1)} %get-tuple-element.73), channel_id=1, source_target_pairs={{0,3},{1,2},{2,1},{3,0},{4,7},{5,6},{6,5},{7,4},{8,11},{9,10},{10,... | collective-permute-start | bytes 786440 | tf_op jit(solution)/shard_map/ppermute | solution.py:471
  79.0 2.8 %collective-permute-start.4 = (f32[2,128,256]{2,1,0:T(8,128)S(1)}, f32[2,128,256]{2,1,0:T(8,128)S(1)}, u32[]{:S(2)}, u32[]{:S(2)}) collective-permute-start(f32[2,128,256]{2,1,0:T(8,128)S(1)} %get-tuple-element.74), channel_id=1, source_target_pairs={{0,1},{1,0},{2,3},{3,2},{4,5},{5,4},{6,7},{7,6},{8,9},{9,8},{10,11... | collective-permute-start | bytes 786440 | tf_op jit(solution)/shard_map/ppermute | solution.py:471
  81.8 6.6 %collective-permute-done.3.got3_ref = f32[2,128,256]{2,1,0:T(8,128)S(1)} collective-permute-done((f32[2,128,256]{2,1,0:T(8,128)S(1)}, f32[2,128,256]{2,1,0:T(8,128)S(1)}, u32[]{:S(2)}, u32[]{:S(2)}) %collective-permute-start.3) | collective-permute-done | bytes 262176 | tf_op jit(solution)/shard_map/ppermute | solution.py:471
  88.4 0.9 collective-permute-done.4.got1_ref
  89.4 2.9 %collective-permute-start.5 = (f32[4,128,256]{2,1,0:T(8,128)S(1)}, f32[4,128,256]{2,1,0:T(8,128)S(1)}, u32[]{:S(2)}, u32[]{:S(2)}) collective-permute-start(f32[4,128,256]{2,1,0:T(8,128)S(1)} %get-tuple-element.75), channel_id=1, source_target_pairs={{0,1},{1,0},{2,3},{3,2},{4,5},{5,4},{6,7},{7,6},{8,9},{9,8},{10,11... | collective-permute-start | bytes 1572872 | tf_op jit(solution)/shard_map/ppermute | solution.py:471
  92.3 4.1 %collective-permute-start.6 = (f32[4,128,256]{2,1,0:T(8,128)S(1)}, f32[4,128,256]{2,1,0:T(8,128)S(1)}, u32[]{:S(2)}, u32[]{:S(2)}) collective-permute-start(f32[4,128,256]{2,1,0:T(8,128)S(1)} %get-tuple-element.76), channel_id=1, source_target_pairs={{0,3},{1,2},{2,1},{3,0},{4,7},{5,6},{6,5},{7,4},{8,11},{9,10},{10,... | collective-permute-start | bytes 1572872 | tf_op jit(solution)/shard_map/ppermute | solution.py:471
  97.1 2.6 %shard_map.158 = (bf16[8,128,256]{2,1,0:T(8,128)(2,1)S(1)}, bf16[8,128,256]{2,1,0:T(8,128)(2,1)S(1)}, f32[8,2,256]{2,1,0:T(2,128)}, f32[16,8,128]{2,1,0:T(8,128)S(1)}) custom-call(f32[16,128,128]{2,1,0:T(8,128)S(1)} %copy-done.2, f32[104,256]{1,0:T(8,128)S(1)} %copy-done.7, bf16[8,128,256]{2,1,0:T(8,128)(2,1)S(1)} %copy-done, ...), custom_call_target="tpu_custom_call" | custom-call | flops 1000000000 | bytes 4194304 | tf_op jit(solution)/shard_map/pallas_call | solution.py:402
  99.7 0.8 copy-done.12
  100.4 10.4 %all_to_all.20.got_ref = f32[16,8,128]{2,1,0:T(8,128)S(1)} all-to-all(f32[16,8,128]{2,1,0:T(8,128)S(1)} %get-tuple-element.80), channel_id=1, replica_groups=mesh['seq'=16,'dp'=8,'mp'=4] {'seq'}, dimensions={0} | all-to-all | bytes 131072 | tf_op jit(solution)/shard_map/all_to_all | solution.py:479
  111.5 7.1 %all-to-all-start.3 = ((f32[8,8,128]{2,1,0:T(8,128)}), f32[8,8,128]{2,1,0:T(8,128)S(1)}, u32[]{:S(2)}, u32[]{:S(2)}) async-start(f32[8,8,128]{2,1,0:T(8,128)} %shard_map.161), calls=%async_computation.3 | async-start | bytes 65536 | tf_op jit(solution)/shard_map/all_to_all | solution.py:498
  118.6 1.0 copy-done.13
  119.6 1.4 %shard_map.159 = (bf16[256,8,128]{2,1,0:T(8,128)(2,1)}, bf16[256,8,128]{2,1,0:T(8,128)(2,1)}) custom-call(bf16[8,128,256]{2,1,0:T(8,128)(2,1)S(1)} %get-tuple-element.67.out_in_ref, bf16[8,128,256]{2,1,0:T(8,128)(2,1)S(1)} %copy-done.13), custom_call_target="tpu_custom_call" | custom-call | flops 1000000000 | bytes 4194304 | tf_op jit(solution)/shard_map/pallas_call | solution.py:402
  121.0 5.6 %all-to-all-done.3.got_ref = f32[8,8,128]{2,1,0:T(8,128)S(1)} async-done(((f32[8,8,128]{2,1,0:T(8,128)}), f32[8,8,128]{2,1,0:T(8,128)S(1)}, u32[]{:S(2)}, u32[]{:S(2)}) %all-to-all-start.3) | async-done | bytes 32800 | tf_op jit(solution)/shard_map/all_to_all | solution.py:498
  126.6 0.6 shard_map.162
  127.2 1.0 shard_map.160
  (29 shorter events, 1.4 us)
Async XLA Ops:
  4.5 4.1 %collective-permute-start = (f32[8,136,128]{2,1,0:T(8,128)}, f32[8,136,128]{2,1,0:T(8,128)S(1)}, u32[]{:S(2)}, u32[]{:S(2)}) collective-permute-start(f32[8,136,128]{2,1,0:T(8,128)} %get-tuple-element.47), channel_id=1, source_target_pairs={{0,32},{32,0},{64,96},{96,64},{128,160},{160,128},{192,224},{224,1... | collective-permute-start | bytes 1671176 | tf_op jit(solution)/shard_map/ppermute | solution.py:447
  8.6 1.1 copy-start.10
  10.5 10.5 %copy-start.11 = (f32[8,136,128]{2,1,0:T(8,128)S(1)}, f32[8,136,128]{2,1,0:T(8,128)}, u32[]{:S(2)}) copy-start(f32[8,136,128]{2,1,0:T(8,128)} %get-tuple-element.46.keep_ref) | copy-start | bytes 1671172
  10.5 28.9 %all-to-all-start = ((f32[8,136,128]{2,1,0:T(8,128)}), f32[8,136,128]{2,1,0:T(8,128)S(1)}, u32[]{:S(2)}, u32[]{:S(2)}) async-start(f32[8,136,128]{2,1,0:T(8,128)} %shard_map.153), calls=%async_computation | async-start | bytes 1114112 | tf_op jit(solution)/shard_map/all_to_all | solution.py:436
  21.0 49.9 %collective-permute-start.2 = (f32[8,136,128]{2,1,0:T(8,128)S(1)}, f32[8,136,128]{2,1,0:T(8,128)S(1)}, u32[]{:S(2)}, u32[]{:S(2)}) collective-permute-start(f32[8,136,128]{2,1,0:T(8,128)S(1)} %copy-done.11), channel_id=1, source_target_pairs={{0,32},{32,0},{64,96},{96,64},{128,160},{160,128},{192,224},{224,1... | collective-permute-start | bytes 1671176 | tf_op jit(solution)/shard_map/ppermute | solution.py:452
  40.3 21.4 %all-to-all-start.1 = ((f32[8,128,128]{2,1,0:T(8,128)}), f32[8,128,128]{2,1,0:T(8,128)S(1)}, u32[]{:S(2)}, u32[]{:S(2)}) async-start(f32[8,128,128]{2,1,0:T(8,128)} %shard_map.154), calls=%async_computation.1 | async-start | bytes 1048576 | tf_op jit(solution)/shard_map/all_to_all | solution.py:436
  61.7 9.2 %collective-permute-start.1 = (f32[8,128,128]{2,1,0:T(8,128)S(1)}, f32[8,128,128]{2,1,0:T(8,128)S(1)}, u32[]{:S(2)}, u32[]{:S(2)}) collective-permute-start(f32[8,128,128]{2,1,0:T(8,128)S(1)} %all-to-all-done.1.ends_mine), channel_id=1, source_target_pairs={{0,32},{32,0},{64,96},{96,64},{128,160},{160,128},{192,224},{224,1... | collective-permute-start | bytes 1572872 | tf_op jit(solution)/shard_map/ppermute | solution.py:451
  63.6 7.3 %copy-start.7 = (f32[104,256]{1,0:T(8,128)S(1)}, f32[104,256]{1,0:T(8,128)}, u32[]{:S(2)}) copy-start(f32[104,256]{1,0:T(8,128)} %get-tuple-element.48.rows_ref) | copy-start | bytes 319492
  70.9 1.0 copy-start
  72.0 1.0 copy-start.1
  73.0 23.4 %copy-start.3 = (f32[8,128,256]{2,1,0:T(8,128)S(1)}, f32[8,128,256]{2,1,0:T(8,128)}, u32[]{:S(2)}) copy-start(f32[8,128,256]{2,1,0:T(8,128)} %get-tuple-element.64.yt_ref) | copy-start | bytes 3145732
  73.0 23.4 %copy-start.4 = (f32[8,128,256]{2,1,0:T(8,128)S(1)}, f32[8,128,256]{2,1,0:T(8,128)}, u32[]{:S(2)}) copy-start(f32[8,128,256]{2,1,0:T(8,128)} %get-tuple-element.65.dxt_ref) | copy-start | bytes 3145732
  73.0 23.4 %copy-start.6 = (bf16[8,128,256]{2,1,0:T(8,128)(2,1)S(1)}, bf16[8,128,256]{2,1,0:T(8,128)(2,1)}, u32[]{:S(2)}) copy-start(bf16[8,128,256]{2,1,0:T(8,128)(2,1)} %get-tuple-element.63.ct_ref) | copy-start | bytes 1572868
  76.5 20.0 %copy-start.2 = (f32[16,128,128]{2,1,0:T(8,128)S(1)}, f32[16,128,128]{2,1,0:T(8,128)}, u32[]{:S(2)}) copy-start(f32[16,128,128]{2,1,0:T(8,128)} %get-tuple-element.61.states_ref) | copy-start | bytes 3145732
  76.5 11.9 %collective-permute-start.3 = (f32[2,128,256]{2,1,0:T(8,128)S(1)}, f32[2,128,256]{2,1,0:T(8,128)S(1)}, u32[]{:S(2)}, u32[]{:S(2)}) collective-permute-start(f32[2,128,256]{2,1,0:T(8,128)S(1)} %get-tuple-element.73), channel_id=1, source_target_pairs={{0,3},{1,2},{2,1},{3,0},{4,7},{5,6},{6,5},{7,4},{8,11},{9,10},{10,... | collective-permute-start | bytes 786440 | tf_op jit(solution)/shard_map/ppermute | solution.py:471
  79.0 10.3 %collective-permute-start.4 = (f32[2,128,256]{2,1,0:T(8,128)S(1)}, f32[2,128,256]{2,1,0:T(8,128)S(1)}, u32[]{:S(2)}, u32[]{:S(2)}) collective-permute-start(f32[2,128,256]{2,1,0:T(8,128)S(1)} %get-tuple-element.74), channel_id=1, source_target_pairs={{0,1},{1,0},{2,3},{3,2},{4,5},{5,4},{6,7},{7,6},{8,9},{9,8},{10,11... | collective-permute-start | bytes 786440 | tf_op jit(solution)/shard_map/ppermute | solution.py:471
  89.3 7.2 %copy-start.5 = (bf16[8,128,256]{2,1,0:T(8,128)(2,1)S(1)}, bf16[8,128,256]{2,1,0:T(8,128)(2,1)}, u32[]{:S(2)}) copy-start(bf16[8,128,256]{2,1,0:T(8,128)(2,1)} %get-tuple-element.62.bt_ref) | copy-start | bytes 1572868
  89.3 7.2 %copy-start.9 = (f32[8,2]{0,1:T(2,128)S(1)}, f32[8,2]{0,1:T(2,128)}, u32[]{:S(2)}) copy-start(f32[8,2]{0,1:T(2,128)} %param.16) | copy-start | bytes 196
  89.4 37.8 %collective-permute-start.5 = (f32[4,128,256]{2,1,0:T(8,128)S(1)}, f32[4,128,256]{2,1,0:T(8,128)S(1)}, u32[]{:S(2)}, u32[]{:S(2)}) collective-permute-start(f32[4,128,256]{2,1,0:T(8,128)S(1)} %get-tuple-element.75), channel_id=1, source_target_pairs={{0,1},{1,0},{2,3},{3,2},{4,5},{5,4},{6,7},{7,6},{8,9},{9,8},{10,11... | collective-permute-start | bytes 1572872 | tf_op jit(solution)/shard_map/ppermute | solution.py:471
  92.3 34.9 %collective-permute-start.6 = (f32[4,128,256]{2,1,0:T(8,128)S(1)}, f32[4,128,256]{2,1,0:T(8,128)S(1)}, u32[]{:S(2)}, u32[]{:S(2)}) collective-permute-start(f32[4,128,256]{2,1,0:T(8,128)S(1)} %get-tuple-element.76), channel_id=1, source_target_pairs={{0,3},{1,2},{2,1},{3,0},{4,7},{5,6},{6,5},{7,4},{8,11},{9,10},{10,... | collective-permute-start | bytes 1572872 | tf_op jit(solution)/shard_map/ppermute | solution.py:471
  96.4 0.7 copy-start.8
  99.7 0.8 copy-start.12
  111.5 15.1 %all-to-all-start.3 = ((f32[8,8,128]{2,1,0:T(8,128)}), f32[8,8,128]{2,1,0:T(8,128)S(1)}, u32[]{:S(2)}, u32[]{:S(2)}) async-start(f32[8,8,128]{2,1,0:T(8,128)} %shard_map.161), calls=%async_computation.3 | async-start | bytes 65536 | tf_op jit(solution)/shard_map/all_to_all | solution.py:498
  118.6 1.0 copy-start.13
